TPU v7x, 256 devices: a whole 4x4x8 slice. The times are simulated.
256 devices in a mesh: shuf: 4 (over y_lo, core), key: 64 (over x, z, y_hi).
Axes of the slice: x: 4, y: 4 (y_hi: 2, y_lo: 2; y = y_hi * 2 + y_lo), z: 8, core: 2. Of those that a mesh axis runs over, the one named last changes fastest.
Arguments:
- embeddings: bfloat16 [32768, 1024], P(('shuf', 'key')), may hold values from -200 to 200
- labels: int32 [32768], P(('shuf', 'key')), may hold values from 0 to 2047
- order: int32 [256, 128], P(('shuf', 'key')), may hold values from 0 to 127, each once within a row
- head_weight: bfloat16 [1024, 512], replicated, may hold values from -0.1875 to 0.1875
Outputs:
- grad_embeddings: bfloat16 [32768, 1024], P(('shuf', 'key'))
- grad_head: float32 [1024, 512], P('key')
All inputs are finite; a program needn't handle non-finite values.
Results may differ from a plain program's by a relative error of at most 0.0075.
Values may be sent and summed in bfloat16 or wider, within the bound.
No kernel may reach another device: no remote copies, remote signals or barrier semaphores. Data moves between devices by JAX's collectives and lax.ppermute only.
A program may use at most 64 MiB of HBM per device.

v0:
```python
import jax
import jax.numpy as jnp
from jax import lax
from jax.sharding import Mesh, PartitionSpec as P

exponent_divisor = 0.1
loss_scale = 64.0
epsilon = 1e-06
AXES = ("yl", "c", "x", "zh", "zl", "yh")
KEY = ("x", "zh", "zl", "yh")
LABEL_ROWS = 16
f32 = jnp.float32
bf16 = jnp.bfloat16


def shift(value, axis, size, distance):
    distance %= size
    if distance == 0:
        return value
    return lax.ppermute(value, axis, [(i, (i + distance) % size) for i in range(size)])


def shift_y(value, distance):
    if distance % 4 == 0:
        return value
    seat = [y % 2 * 2 + y // 2 for y in range(4)]
    return lax.ppermute(
        value, ("yl", "yh"), [(seat[y], seat[(y + distance) % 4]) for y in range(4)]
    )


def unpack(stack, rows):
    normed = stack[:, :rows].reshape(-1, stack.shape[2])
    high = stack[:, rows, :rows].astype(jnp.int32)
    low = stack[:, rows, rows : 2 * rows].astype(jnp.int32)
    return (normed, (high * 64 + low).reshape(-1))


def body(embeddings, labels, order, head_weight):
    rows, width = embeddings.shape
    proj = head_weight.shape[1]
    zh = lax.axis_index("zh")
    share = rows // 4
    doubled = jnp.concatenate([order[0], order[0]])
    routing = lax.dynamic_slice_in_dim(doubled, zh * share, rows)
    with jax.named_scope("route_out"):
        pick = (routing[:, None] == jnp.arange(rows, dtype=jnp.int32)[None, :]).astype(bf16)
        lane = jnp.arange(128, dtype=jnp.int32)[None, :]
        tag = jnp.where(
            lane == 0, (labels // 64)[:, None], jnp.where(lane == 1, (labels % 64)[:, None], 0)
        ).astype(bf16)
        tagged = jnp.concatenate([embeddings, tag], axis=1)
        sent = jnp.dot(pick, tagged, preferred_element_type=f32).astype(bf16)
        sent = sent.reshape(4, share, width + 128)
        got = jnp.concatenate([shift(sent[d], "zh", 4, d) for d in range(4)], axis=0)
    group_rows = got[:, :width]

    def project(values):
        projected = jnp.dot(values, head_weight, preferred_element_type=f32)
        norm = jnp.sqrt(jnp.sum(projected * projected, axis=1, keepdims=True) + epsilon)
        return (projected / norm, norm)

    with jax.named_scope("project"):
        direction, row_norm = project(group_rows)
        normed = direction.astype(bf16)
        label_line = jnp.concatenate(
            [got[:, width], got[:, width + 1], jnp.zeros((proj - 2 * rows,), bf16)]
        )
        label_block = jnp.broadcast_to(label_line[None, :], (LABEL_ROWS, proj))
        packet = jnp.concatenate([normed, label_block], axis=0)
    with jax.named_scope("gather_sets"):
        across_x = jnp.stack([shift(got, "x", 4, d) for d in range(4)])
        across_y = [shift_y(packet, d) for d in range(4)]
        set_b = jnp.stack([shift(block, "zl", 2, dz) for block in across_y for dz in range(2)])
        normed_b, labels_b = unpack(set_b, rows)
        set_a = jnp.concatenate([across_x, shift(across_x, "c", 2, 1)], axis=0)
        set_a = set_a.reshape(-1, width + 128)
        rows_a = set_a[:, :width]
        high = set_a[:, width].astype(jnp.int32)
        labels_a = high * 64 + set_a[:, width + 1].astype(jnp.int32)
        direction_a, norm_a = project(rows_a)
        normed_a = direction_a.astype(bf16)
    with jax.named_scope("scores"):
        total = normed_a.shape[0]
        scores = (
            lax.dot_general(
                normed_a, normed_b, (((1,), (1,)), ((), ())), preferred_element_type=f32
            )
            / exponent_divisor
        )
        row = jnp.arange(total, dtype=jnp.int32)
        itself = jnp.logical_and(row[:, None] == row[None, :], (row < rows)[:, None])
        exponent = jnp.where(itself, 0.0, jnp.exp(scores))
        positive = jnp.logical_and(
            labels_a[:, None] == labels_b[None, :], jnp.logical_not(itself)
        ).astype(f32)
        sums_a = jnp.stack([jnp.sum(exponent, axis=1), jnp.sum(positive, axis=1)])
        sums_b = jnp.stack([jnp.sum(exponent, axis=0), jnp.sum(positive, axis=0)])
    with jax.named_scope("totals"):
        sums_a = sums_a.reshape(2, 2, 4, rows)
        sums_a = sums_a + jnp.roll(shift(sums_a, "c", 2, 1), 1, axis=1)
        sums_a = sum([jnp.roll(shift(sums_a, "x", 4, d), d, axis=2) for d in range(4)])
        sums_b = sums_b.reshape(2, 4, 2, rows)
        sums_b = sums_b + jnp.roll(shift(sums_b, "zl", 2, 1), 1, axis=2)
        sums_b = sum([jnp.roll(shift_y(sums_b, d), d, axis=1) for d in range(4)])

        def weights(sums):
            totals, counts = sums.reshape(2, total)
            floor_count = jnp.maximum(counts, 1.0)
            return (loss_scale * counts / (floor_count * totals), loss_scale / floor_count)

        soft_a, pos_a = weights(sums_a)
        soft_b, pos_b = weights(sums_b)
    with jax.named_scope("pull"):
        half = total // 2

        def pull_rows(start):
            take = slice(start, start + half)
            coefficient = (
                (soft_a[take, None] + soft_b[None, :]) * exponent[take]
                - (pos_a[take, None] + pos_b[None, :]) * positive[take]
            ).astype(bf16)
            part = jnp.dot(coefficient, normed_b, preferred_element_type=f32)
            return part.reshape(4, rows, proj)

        pull_far = pull_rows(half)
        crossing = shift(pull_far, "c", 2, 1)
        pull_near = lax.optimization_barrier(pull_rows(0))

    def to_slopes(pull_grad, unit, norm):
        along = jnp.sum(unit * pull_grad, axis=1, keepdims=True)
        return ((pull_grad - unit * along) / norm).astype(bf16)

    with jax.named_scope("head"):
        pull_part = jnp.concatenate([pull_near, pull_far]).reshape(total, proj)
        slopes_part = to_slopes(pull_part / exponent_divisor, direction_a, norm_a)
        part = lax.dot_general(
            rows_a, slopes_part, (((0,), (0,)), ((), ())), preferred_element_type=f32
        )
        part = part.reshape(64, 2, width // 128, proj)
        core = lax.axis_index("c")
        kept = lax.dynamic_index_in_dim(part, core, axis=1, keepdims=False)
        given = lax.dynamic_index_in_dim(part, 1 - core, axis=1, keepdims=False)
        part = (kept + shift(given.astype(bf16), "c", 2, 1).astype(f32)).astype(bf16)
        spread = lax.all_to_all(part, KEY, split_axis=0, concat_axis=0, tiled=True)
        piece = jnp.sum(spread.astype(f32), axis=0)
        piece = piece + shift(piece, "yl", 2, 1)
        grad_head = lax.all_gather(piece, "c", axis=0, tiled=True)
    with jax.named_scope("slopes"):
        pull = pull_near + crossing
        parts = [shift(pull[d].astype(bf16), "x", 4, -d).astype(f32) for d in range(1, 4)]
        pull_grad = (pull[0] + sum(parts)) / exponent_divisor
        slopes = to_slopes(pull_grad, direction, row_norm)
    with jax.named_scope("route_back"):
        blocks = slopes.reshape(4, share, proj)
        returned = jnp.concatenate([shift(blocks[d], "zh", 4, -d) for d in range(4)], axis=0)
        own = lax.dot_general(
            pick, returned, (((0,), (0,)), ((), ())), preferred_element_type=f32
        ).astype(bf16)
        grad_embeddings = lax.dot_general(
            own, head_weight, (((1,), (1,)), ((), ())), preferred_element_type=f32
        ).astype(bf16)
    return (grad_embeddings, grad_head / loss_scale)


def solution(mesh):
    split = Mesh(mesh.devices.reshape(2, 2, 4, 4, 2, 2), AXES)
    return jax.shard_map(
        body,
        mesh=split,
        in_specs=(P(AXES, None), P(AXES), P(AXES, None), P()),
        out_specs=(P(AXES, None), P(KEY, None)),
        check_vma=False,
    )
```

profile of v0, /device:TPU:1, one launch (start us, length us, event | category | flops | bytes accessed | tf_op | source)
XLA Modules:
  0.0 137.2 jit_solution(9923911454990041922)
XLA Ops:
  3.5 3.9 %collective-permute-start = (bf16[32,1152]{1,0:T(8,128)(2,1)S(1)}, bf16[32,1152]{1,0:T(8,128)(2,1)S(1)}, u32[]{:S(2)}, u32[]{:S(2)}) collective-permute-start(bf16[32,1152]{1,0:T(8,128)(2,1)S(1)} %get-tuple-element.22), channel_id=1, source_target_pairs={{0,4},{4,8},{8,12},{12,0},{1,5},{5,9},{9,13},{13,1},{2,6},{6,10},{... | collective-permute-start | bytes 221192 | tf_op jit(solution)/shard_map/route_out/ppermute | solution.py:20
  7.4 5.1 %collective-permute-start.1 = (bf16[32,1152]{1,0:T(8,128)(2,1)S(1)}, bf16[32,1152]{1,0:T(8,128)(2,1)S(1)}, u32[]{:S(2)}, u32[]{:S(2)}) collective-permute-start(bf16[32,1152]{1,0:T(8,128)(2,1)S(1)} %get-tuple-element.21), channel_id=1, source_target_pairs={{0,8},{4,12},{8,0},{12,4},{1,9},{5,13},{9,1},{13,5},{2,10},{6,14},... | collective-permute-start | bytes 221192 | tf_op jit(solution)/shard_map/route_out/ppermute | solution.py:20
  12.6 2.4 %collective-permute-start.2 = (bf16[32,1152]{1,0:T(8,128)(2,1)S(1)}, bf16[32,1152]{1,0:T(8,128)(2,1)S(1)}, u32[]{:S(2)}, u32[]{:S(2)}) collective-permute-start(bf16[32,1152]{1,0:T(8,128)(2,1)S(1)} %get-tuple-element.20), channel_id=1, source_target_pairs={{0,12},{4,0},{8,4},{12,8},{1,13},{5,1},{9,5},{13,9},{2,14},{6,2},{... | collective-permute-start | bytes 221192 | tf_op jit(solution)/shard_map/route_out/ppermute | solution.py:20
  14.9 2.0 %collective-permute-done.1 = bf16[32,1152]{1,0:T(8,128)(2,1)S(1)} collective-permute-done((bf16[32,1152]{1,0:T(8,128)(2,1)S(1)}, bf16[32,1152]{1,0:T(8,128)(2,1)S(1)}, u32[]{:S(2)}, u32[]{:S(2)}) %collective-permute-start.1) | collective-permute-done | bytes 73760 | tf_op jit(solution)/shard_map/route_out/ppermute | solution.py:20
  16.9 3.9 %collective-permute-done.2 = bf16[32,1152]{1,0:T(8,128)(2,1)S(1)} collective-permute-done((bf16[32,1152]{1,0:T(8,128)(2,1)S(1)}, bf16[32,1152]{1,0:T(8,128)(2,1)S(1)}, u32[]{:S(2)}, u32[]{:S(2)}) %collective-permute-start.2) | collective-permute-done | bytes 73760 | tf_op jit(solution)/shard_map/route_out/ppermute | solution.py:20
  22.2 2.5 %collective-permute-start.4 = (bf16[128,1152]{1,0:T(8,128)(2,1)S(1)}, bf16[128,1152]{1,0:T(8,128)(2,1)S(1)}, u32[]{:S(2)}, u32[]{:S(2)}) collective-permute-start(bf16[128,1152]{1,0:T(8,128)(2,1)S(1)} %get-tuple-element.18), channel_id=1, source_target_pairs={{0,32},{16,48},{32,0},{48,16},{1,33},{17,49},{33,1},{49,17},{2,34}... | collective-permute-start | bytes 884744 | tf_op jit(solution)/shard_map/gather_sets/ppermute | solution.py:20
  28.1 2.9 %collective-permute-done.7 = bf16[144,512]{1,0:T(8,128)(2,1)S(1)} collective-permute-done((bf16[144,512]{1,0:T(8,128)(2,1)S(1)}, bf16[144,512]{1,0:T(8,128)(2,1)S(1)}, u32[]{:S(2)}, u32[]{:S(2)}) %collective-permute-start.7) | collective-permute-done | bytes 147488 | tf_op jit(solution)/shard_map/gather_sets/ppermute | solution.py:20
  30.9 2.9 %collective-permute-start.10 = (bf16[144,512]{1,0:T(8,128)(2,1)S(1)}, bf16[144,512]{1,0:T(8,128)(2,1)S(1)}, u32[]{:S(2)}, u32[]{:S(2)}) collective-permute-start(bf16[144,512]{1,0:T(8,128)(2,1)S(1)} %pad_maximum_fusion.2), channel_id=1, source_target_pairs={{0,1},{128,129},{1,0},{129,128},{2,3},{130,131},{3,2},{131,130},{4... | collective-permute-start | bytes 442376 | tf_op jit(solution)/shard_map/gather_sets/ppermute | solution.py:27
  34.7 2.1 %collective-permute-done.10 = bf16[144,512]{1,0:T(8,128)(2,1)S(1)} collective-permute-done((bf16[144,512]{1,0:T(8,128)(2,1)S(1)}, bf16[144,512]{1,0:T(8,128)(2,1)S(1)}, u32[]{:S(2)}, u32[]{:S(2)}) %collective-permute-start.10) | collective-permute-done | bytes 147488 | tf_op jit(solution)/shard_map/gather_sets/ppermute | solution.py:27
  40.7 3.9 %collective-permute-start.6 = (bf16[4,128,1152]{2,1,0:T(8,128)(2,1)S(1)}, bf16[4,128,1152]{2,1,0:T(8,128)(2,1)S(1)}, u32[]{:S(2)}, u32[]{:S(2)}) collective-permute-start(bf16[4,128,1152]{2,1,0:T(8,128)(2,1)S(1)} %pad_maximum_fusion), channel_id=1, source_target_pairs={{0,64},{64,0},{1,65},{65,1},{2,66},{66,2},{3,67},{67,3},{4,68},{68... | collective-permute-start | bytes 3538952 | tf_op jit(solution)/shard_map/gather_sets/ppermute | solution.py:20
  44.8 2.1 %collective-permute-done.13 = bf16[144,512]{1,0:T(8,128)(2,1)S(1)} collective-permute-done((bf16[144,512]{1,0:T(8,128)(2,1)S(1)}, bf16[144,512]{1,0:T(8,128)(2,1)S(1)}, u32[]{:S(2)}, u32[]{:S(2)}) %collective-permute-start.13) | collective-permute-done | bytes 147488 | tf_op jit(solution)/shard_map/gather_sets/ppermute | solution.py:20
  53.1 2.2 %fusion.9 = (f32[1024]{0:T(1024)S(1)}, f32[1024]{0:T(1024)S(1)}) fusion(pred[1024]{0:T(1024)(128)(4,1)S(1)} %iota_compare_fusion.5, s32[1024]{0:T(1024)S(1)} %bitcast.109, s32[1024]{0:T(1024)S(1)} %bitcast.111), kind=kLoop, calls=%fused_computation.20 | loop fusion | flops 8386560 | bytes 17408 | tf_op jit(solution)/shard_map/scores/reduce_sum | solution.py:97
  56.6 1.9 %fusion.58 = (f32[1024]{0:T(1024)S(1)}, f32[1024]{0:T(1024)S(1)}, f32[1024,1024]{1,0:T(8,128)S(1)}) fusion(bf16[1024,512]{1,0:T(8,128)(2,1)S(1)} %bitcast.89, f32[1024,512]{0,1:T(8,128)S(1)} %get-tuple-element.48, f32[1024]{0:T(1024)S(1)} %add_sqrt_fusion, pred[1024]{0:T(1024)(128)(4,1)S(1)} %iota_compare_fusion.5), kind=kOutput, calls=%fused_computation.124 | convolution fusion | flops 1081079808 | bytes 7353344 | tf_op jit(solution)/shard_map/scores/dot_general | solution.py:86
  58.6 3.4 %collective-permute-start.14 = (f32[2,2,4,128]{3,2,1,0:T(4,128)S(1)}, f32[2,2,4,128]{3,2,1,0:T(4,128)S(1)}, u32[]{:S(2)}, u32[]{:S(2)}) collective-permute-start(f32[2,2,4,128]{3,2,1,0:T(4,128)S(1)} %pad_maximum_fusion.3), channel_id=1, source_target_pairs={{0,64},{64,0},{1,65},{65,1},{2,66},{66,2},{3,67},{67,3},{4,68},{68... | collective-permute-start | bytes 24584 | tf_op jit(solution)/shard_map/totals/ppermute | solution.py:20
  62.1 2.2 %collective-permute-start.20 = (f32[2,4,2,128]{3,2,1,0:T(2,128)S(1)}, f32[2,4,2,128]{3,2,1,0:T(2,128)S(1)}, u32[]{:S(2)}, u32[]{:S(2)}) collective-permute-start(f32[2,4,2,128]{3,2,1,0:T(2,128)S(1)} %maximum_add_fusion.2), channel_id=1, source_target_pairs={{0,1},{128,129},{1,0},{129,128},{2,3},{130,131},{3,2},{131,130},{4... | collective-permute-start | bytes 24584 | tf_op jit(solution)/shard_map/totals/ppermute | solution.py:27
  67.3 2.3 %collective-permute-start.17 = (f32[2,2,4,128]{3,2,1,0:T(4,128)S(1)}, f32[2,2,4,128]{3,2,1,0:T(4,128)S(1)}, u32[]{:S(2)}, u32[]{:S(2)}) collective-permute-start(f32[2,2,4,128]{3,2,1,0:T(4,128)S(1)} %maximum_add_fusion), channel_id=1, source_target_pairs={{0,48},{16,0},{32,16},{48,32},{1,49},{17,1},{33,17},{49,33},{2,50}... | collective-permute-start | bytes 24584 | tf_op jit(solution)/shard_map/totals/ppermute | solution.py:20
  71.1 2.2 %collective-permute-done.15 = f32[2,2,4,128]{3,2,1,0:T(4,128)S(1)} collective-permute-done((f32[2,2,4,128]{3,2,1,0:T(4,128)S(1)}, f32[2,2,4,128]{3,2,1,0:T(4,128)S(1)}, u32[]{:S(2)}, u32[]{:S(2)}) %collective-permute-start.15) | collective-permute-done | bytes 8224 | tf_op jit(solution)/shard_map/totals/ppermute | solution.py:20
  76.9 5.8 %collective-permute-start.22 = (f32[4,128,512]{2,1,0:T(8,128)}, f32[4,128,512]{2,1,0:T(8,128)}, u32[]{:S(2)}, u32[]{:S(2)}) collective-permute-start(f32[4,128,512]{2,1,0:T(8,128)} %fusion.68), channel_id=1, source_target_pairs={{0,64},{64,0},{1,65},{65,1},{2,66},{66,2},{3,67},{67,3},{4,68},{68... | collective-permute-start | bytes 3145736 | tf_op jit(solution)/shard_map/pull/ppermute | solution.py:20
  82.7 2.8 %maximum_multiply_fusion = f32[8,128,512]{2,1,0:T(8,128)} fusion(f32[4,128,512]{2,1,0:T(8,128)} %fusion.68, f32[4,128,512]{2,1,0:T(8,128)S(1)} %fusion.67), kind=kLoop, calls=%fused_computation.15 | loop fusion | flops 1048576 | bytes 4194304 | tf_op jit(solution)/shard_map/head/div | solution.py:136
  85.6 1.9 %copy.10 = f32[1024,512]{0,1:T(8,128)S(1)} copy(f32[1024,512]{1,0:T(8,128)} %bitcast.81) | data formatting | bytes 4194304 | tf_op jit(solution)/shard_map/head/div | solution.py:136
  87.5 2.0 %multiply_reduce_fusion = f32[1024]{0:T(1024)S(1)} fusion(f32[1024,512]{0,1:T(8,128)S(1)} %copy.10, f32[1024,512]{0,1:T(8,128)} %copy-done.3, f32[1024]{0:T(1024)S(1)} %add_sqrt_fusion), kind=kLoop, calls=%fused_computation.17 | loop fusion | flops 1571840 | bytes 4202496 | tf_op jit(solution)/shard_map/head/reduce_sum | solution.py:131
  89.7 2.9 %fusion.10 = f32[1024,512]{1,0:T(8,128)S(1)} fusion(bf16[1024,1152]{1,0:T(8,128)(2,1)} %bitcast.94, f32[1024,512]{0,1:T(8,128)S(1)} %copy.10, f32[1024]{0:T(1024)S(1)} %multiply_reduce_fusion, f32[1024]{0:T(1024)S(1)} %add_sqrt_fusion, f32[1024,512]{0,1:T(8,128)S(1)} %copy-done.4), kind=kOutput, calls=%fused_computation.21 | convolution fusion | flops 1076363264 | bytes 8396800 | tf_op jit(solution)/shard_map/head/dot_general | solution.py:137
  96.1 2.2 %fusion.14 = bf16[64,8,512]{2,1,0:T(8,128)(2,1)} fusion(bf16[64,8,512]{2,1,0:T(8,128)(2,1)S(1)} %collective-permute-done.29, f32[64,2,8,512]{3,2,1,0:T(8,128)} %bitcast.86, s32[]{:T(128)S(6)} %select_n.40), kind=kLoop, calls=%fused_computation.29 | loop fusion | flops 786432 | bytes 2097156 | tf_op jit(solution)/shard_map/head/convert_element_type | solution.py:144
  98.3 5.3 %all-to-all-start = ((bf16[64,8,512]{2,1,0:T(8,128)(2,1)}), bf16[64,8,512]{2,1,0:T(8,128)(2,1)S(1)}, u32[]{:S(2)}, u32[]{:S(2)}) async-start(bf16[64,8,512]{2,1,0:T(8,128)(2,1)} %fusion.14), calls=%async_computation | async-start | bytes 1048576 | tf_op jit(solution)/shard_map/head/all_to_all | solution.py:145
  105.2 2.5 %collective-permute-start.23 = (bf16[128,512]{1,0:T(8,128)(2,1)S(1)}, bf16[128,512]{1,0:T(8,128)(2,1)S(1)}, u32[]{:S(2)}, u32[]{:S(2)}) collective-permute-start(bf16[128,512]{1,0:T(8,128)(2,1)S(1)} %get-tuple-element.14), channel_id=1, source_target_pairs={{0,48},{16,0},{32,16},{48,32},{1,49},{17,1},{33,17},{49,33},{2,50}... | collective-permute-start | bytes 393224 | tf_op jit(solution)/shard_map/slopes/ppermute | solution.py:20
  108.7 4.0 %collective-permute-done.23 = bf16[128,512]{1,0:T(8,128)(2,1)S(1)} collective-permute-done((bf16[128,512]{1,0:T(8,128)(2,1)S(1)}, bf16[128,512]{1,0:T(8,128)(2,1)S(1)}, u32[]{:S(2)}, u32[]{:S(2)}) %collective-permute-start.23) | collective-permute-done | bytes 131104 | tf_op jit(solution)/shard_map/slopes/ppermute | solution.py:20
  112.7 3.4 %collective-permute-done.24 = bf16[128,512]{1,0:T(8,128)(2,1)S(1)} collective-permute-done((bf16[128,512]{1,0:T(8,128)(2,1)S(1)}, bf16[128,512]{1,0:T(8,128)(2,1)S(1)}, u32[]{:S(2)}, u32[]{:S(2)}) %collective-permute-start.24) | collective-permute-done | bytes 131104 | tf_op jit(solution)/shard_map/slopes/ppermute | solution.py:20
  116.1 5.6 %collective-permute-done.25 = bf16[128,512]{1,0:T(8,128)(2,1)S(1)} collective-permute-done((bf16[128,512]{1,0:T(8,128)(2,1)S(1)}, bf16[128,512]{1,0:T(8,128)(2,1)S(1)}, u32[]{:S(2)}, u32[]{:S(2)}) %collective-permute-start.25) | collective-permute-done | bytes 131104 | tf_op jit(solution)/shard_map/slopes/ppermute | solution.py:20
  122.0 2.9 %collective-permute-start.26 = (bf16[32,512]{1,0:T(8,128)(2,1)S(1)}, bf16[32,512]{1,0:T(8,128)(2,1)S(1)}, u32[]{:S(2)}, u32[]{:S(2)}) collective-permute-start(bf16[32,512]{1,0:T(8,128)(2,1)S(1)} %get-tuple-element.26), channel_id=1, source_target_pairs={{0,12},{4,0},{8,4},{12,8},{1,13},{5,1},{9,5},{13,9},{2,14},{6,2},{... | collective-permute-start | bytes 98312 | tf_op jit(solution)/shard_map/route_back/ppermute | solution.py:20
  126.4 1.9 %collective-permute-start.28 = (bf16[32,512]{1,0:T(8,128)(2,1)S(1)}, bf16[32,512]{1,0:T(8,128)(2,1)S(1)}, u32[]{:S(2)}, u32[]{:S(2)}) collective-permute-start(bf16[32,512]{1,0:T(8,128)(2,1)S(1)} %get-tuple-element.24), channel_id=1, source_target_pairs={{0,4},{4,8},{8,12},{12,0},{1,5},{5,9},{9,13},{13,1},{2,6},{6,10},{... | collective-permute-start | bytes 98312 | tf_op jit(solution)/shard_map/route_back/ppermute | solution.py:20
  129.2 2.4 %collective-permute-done.27 = bf16[32,512]{1,0:T(8,128)(2,1)S(1)} collective-permute-done((bf16[32,512]{1,0:T(8,128)(2,1)S(1)}, bf16[32,512]{1,0:T(8,128)(2,1)S(1)}, u32[]{:S(2)}, u32[]{:S(2)}) %collective-permute-start.27) | collective-permute-done | bytes 32800 | tf_op jit(solution)/shard_map/route_back/ppermute | solution.py:20
  133.0 3.6 %all_gather.3 = f32[16,512]{1,0:T(8,128)S(1)} all-gather(f32[8,512]{1,0:T(8,128)S(1)} %add.178), channel_id=1, replica_groups=mesh['yl'=2,'c'=2,'x'=4,'zh'=4,'zl'=2,'yh'=2] {'c'}, dimensions={0}, use_global_device_ids=true | all-gather | bytes 49152 | tf_op jit(solution)/shard_map/head/all_gather | solution.py:148
  (130 shorter events, 38.7 us)
Async XLA Ops:
  3.5 11.4 %collective-permute-start = (bf16[32,1152]{1,0:T(8,128)(2,1)S(1)}, bf16[32,1152]{1,0:T(8,128)(2,1)S(1)}, u32[]{:S(2)}, u32[]{:S(2)}) collective-permute-start(bf16[32,1152]{1,0:T(8,128)(2,1)S(1)} %get-tuple-element.22), channel_id=1, source_target_pairs={{0,4},{4,8},{8,12},{12,0},{1,5},{5,9},{9,13},{13,1},{2,6},{6,10},{... | collective-permute-start | bytes 221192 | tf_op jit(solution)/shard_map/route_out/ppermute | solution.py:20
  7.4 9.5 %collective-permute-start.1 = (bf16[32,1152]{1,0:T(8,128)(2,1)S(1)}, bf16[32,1152]{1,0:T(8,128)(2,1)S(1)}, u32[]{:S(2)}, u32[]{:S(2)}) collective-permute-start(bf16[32,1152]{1,0:T(8,128)(2,1)S(1)} %get-tuple-element.21), channel_id=1, source_target_pairs={{0,8},{4,12},{8,0},{12,4},{1,9},{5,13},{9,1},{13,5},{2,10},{6,14},... | collective-permute-start | bytes 221192 | tf_op jit(solution)/shard_map/route_out/ppermute | solution.py:20
  12.6 8.3 %collective-permute-start.2 = (bf16[32,1152]{1,0:T(8,128)(2,1)S(1)}, bf16[32,1152]{1,0:T(8,128)(2,1)S(1)}, u32[]{:S(2)}, u32[]{:S(2)}) collective-permute-start(bf16[32,1152]{1,0:T(8,128)(2,1)S(1)} %get-tuple-element.20), channel_id=1, source_target_pairs={{0,12},{4,0},{8,4},{12,8},{1,13},{5,1},{9,5},{13,9},{2,14},{6,2},{... | collective-permute-start | bytes 221192 | tf_op jit(solution)/shard_map/route_out/ppermute | solution.py:20
  20.9 18.2 %collective-permute-start.3 = (bf16[128,1152]{1,0:T(8,128)(2,1)S(1)}, bf16[128,1152]{1,0:T(8,128)(2,1)S(1)}, u32[]{:S(2)}, u32[]{:S(2)}) collective-permute-start(bf16[128,1152]{1,0:T(8,128)(2,1)S(1)} %get-tuple-element.18), channel_id=1, source_target_pairs={{0,16},{16,32},{32,48},{48,0},{1,17},{17,33},{33,49},{49,1},{2,18}... | collective-permute-start | bytes 884744 | tf_op jit(solution)/shard_map/gather_sets/ppermute | solution.py:20
  22.2 18.4 %collective-permute-start.4 = (bf16[128,1152]{1,0:T(8,128)(2,1)S(1)}, bf16[128,1152]{1,0:T(8,128)(2,1)S(1)}, u32[]{:S(2)}, u32[]{:S(2)}) collective-permute-start(bf16[128,1152]{1,0:T(8,128)(2,1)S(1)} %get-tuple-element.18), channel_id=1, source_target_pairs={{0,32},{16,48},{32,0},{48,16},{1,33},{17,49},{33,1},{49,17},{2,34}... | collective-permute-start | bytes 884744 | tf_op jit(solution)/shard_map/gather_sets/ppermute | solution.py:20
  24.6 15.9 %collective-permute-start.5 = (bf16[128,1152]{1,0:T(8,128)(2,1)S(1)}, bf16[128,1152]{1,0:T(8,128)(2,1)S(1)}, u32[]{:S(2)}, u32[]{:S(2)}) collective-permute-start(bf16[128,1152]{1,0:T(8,128)(2,1)S(1)} %get-tuple-element.18), channel_id=1, source_target_pairs={{0,48},{16,0},{32,16},{48,32},{1,49},{17,1},{33,17},{49,33},{2,50}... | collective-permute-start | bytes 884744 | tf_op jit(solution)/shard_map/gather_sets/ppermute | solution.py:20
  26.5 4.4 %collective-permute-start.7 = (bf16[144,512]{1,0:T(8,128)(2,1)S(1)}, bf16[144,512]{1,0:T(8,128)(2,1)S(1)}, u32[]{:S(2)}, u32[]{:S(2)}) collective-permute-start(bf16[144,512]{1,0:T(8,128)(2,1)S(1)} %pad_maximum_fusion.2), channel_id=1, source_target_pairs={{0,2},{2,0},{1,3},{3,1},{4,6},{6,4},{5,7},{7,5},{8,10},{10,8},{9,1... | collective-permute-start | bytes 442376 | tf_op jit(solution)/shard_map/gather_sets/ppermute | solution.py:20
  26.6 7.2 %collective-permute-start.8 = (bf16[144,512]{1,0:T(8,128)(2,1)S(1)}, bf16[144,512]{1,0:T(8,128)(2,1)S(1)}, u32[]{:S(2)}, u32[]{:S(2)}) collective-permute-start(bf16[144,512]{1,0:T(8,128)(2,1)S(1)} %pad_maximum_fusion.2), channel_id=1, source_target_pairs={{0,128},{128,1},{1,129},{129,0},{2,130},{130,3},{3,131},{131,2},{4... | collective-permute-start | bytes 442376 | tf_op jit(solution)/shard_map/gather_sets/ppermute | solution.py:27
  30.9 5.9 %collective-permute-start.10 = (bf16[144,512]{1,0:T(8,128)(2,1)S(1)}, bf16[144,512]{1,0:T(8,128)(2,1)S(1)}, u32[]{:S(2)}, u32[]{:S(2)}) collective-permute-start(bf16[144,512]{1,0:T(8,128)(2,1)S(1)} %pad_maximum_fusion.2), channel_id=1, source_target_pairs={{0,1},{128,129},{1,0},{129,128},{2,3},{130,131},{3,2},{131,130},{4... | collective-permute-start | bytes 442376 | tf_op jit(solution)/shard_map/gather_sets/ppermute | solution.py:27
  33.9 5.2 %collective-permute-start.12 = (bf16[144,512]{1,0:T(8,128)(2,1)S(1)}, bf16[144,512]{1,0:T(8,128)(2,1)S(1)}, u32[]{:S(2)}, u32[]{:S(2)}) collective-permute-start(bf16[144,512]{1,0:T(8,128)(2,1)S(1)} %pad_maximum_fusion.2), channel_id=1, source_target_pairs={{0,129},{128,0},{1,128},{129,1},{2,131},{130,2},{3,130},{131,3},{4... | collective-permute-start | bytes 442376 | tf_op jit(solution)/shard_map/gather_sets/ppermute | solution.py:27
  36.8 7.9 %collective-permute-start.9 = (bf16[144,512]{1,0:T(8,128)(2,1)S(1)}, bf16[144,512]{1,0:T(8,128)(2,1)S(1)}, u32[]{:S(2)}, u32[]{:S(2)}) collective-permute-start(bf16[144,512]{1,0:T(8,128)(2,1)S(1)} %collective-permute-done.8), channel_id=1, source_target_pairs={{0,2},{2,0},{1,3},{3,1},{4,6},{6,4},{5,7},{7,5},{8,10},{10,8},{9,1... | collective-permute-start | bytes 442376 | tf_op jit(solution)/shard_map/gather_sets/ppermute | solution.py:20
  39.1 5.7 %collective-permute-start.11 = (bf16[144,512]{1,0:T(8,128)(2,1)S(1)}, bf16[144,512]{1,0:T(8,128)(2,1)S(1)}, u32[]{:S(2)}, u32[]{:S(2)}) collective-permute-start(bf16[144,512]{1,0:T(8,128)(2,1)S(1)} %collective-permute-done.10), channel_id=1, source_target_pairs={{0,2},{2,0},{1,3},{3,1},{4,6},{6,4},{5,7},{7,5},{8,10},{10,8},{9,1... | collective-permute-start | bytes 442376 | tf_op jit(solution)/shard_map/gather_sets/ppermute | solution.py:20
  39.1 7.9 %collective-permute-start.13 = (bf16[144,512]{1,0:T(8,128)(2,1)S(1)}, bf16[144,512]{1,0:T(8,128)(2,1)S(1)}, u32[]{:S(2)}, u32[]{:S(2)}) collective-permute-start(bf16[144,512]{1,0:T(8,128)(2,1)S(1)} %collective-permute-done.12), channel_id=1, source_target_pairs={{0,2},{2,0},{1,3},{3,1},{4,6},{6,4},{5,7},{7,5},{8,10},{10,8},{9,1... | collective-permute-start | bytes 442376 | tf_op jit(solution)/shard_map/gather_sets/ppermute | solution.py:20
  40.7 7.4 %collective-permute-start.6 = (bf16[4,128,1152]{2,1,0:T(8,128)(2,1)S(1)}, bf16[4,128,1152]{2,1,0:T(8,128)(2,1)S(1)}, u32[]{:S(2)}, u32[]{:S(2)}) collective-permute-start(bf16[4,128,1152]{2,1,0:T(8,128)(2,1)S(1)} %pad_maximum_fusion), channel_id=1, source_target_pairs={{0,64},{64,0},{1,65},{65,1},{2,66},{66,2},{3,67},{67,3},{4,68},{68... | collective-permute-start | bytes 3538952 | tf_op jit(solution)/shard_map/gather_sets/ppermute | solution.py:20
  58.5 3.5 %collective-permute-start.18 = (f32[2,4,2,128]{3,2,1,0:T(2,128)S(1)}, f32[2,4,2,128]{3,2,1,0:T(2,128)S(1)}, u32[]{:S(2)}, u32[]{:S(2)}) collective-permute-start(f32[2,4,2,128]{3,2,1,0:T(2,128)S(1)} %pad_maximum_fusion.4), channel_id=1, source_target_pairs={{0,2},{2,0},{1,3},{3,1},{4,6},{6,4},{5,7},{7,5},{8,10},{10,8},{9,1... | collective-permute-start | bytes 24584 | tf_op jit(solution)/shard_map/totals/ppermute | solution.py:20
  58.6 8.3 %collective-permute-start.14 = (f32[2,2,4,128]{3,2,1,0:T(4,128)S(1)}, f32[2,2,4,128]{3,2,1,0:T(4,128)S(1)}, u32[]{:S(2)}, u32[]{:S(2)}) collective-permute-start(f32[2,2,4,128]{3,2,1,0:T(4,128)S(1)} %pad_maximum_fusion.3), channel_id=1, source_target_pairs={{0,64},{64,0},{1,65},{65,1},{2,66},{66,2},{3,67},{67,3},{4,68},{68... | collective-permute-start | bytes 24584 | tf_op jit(solution)/shard_map/totals/ppermute | solution.py:20
  62.1 7.6 %collective-permute-start.20 = (f32[2,4,2,128]{3,2,1,0:T(2,128)S(1)}, f32[2,4,2,128]{3,2,1,0:T(2,128)S(1)}, u32[]{:S(2)}, u32[]{:S(2)}) collective-permute-start(f32[2,4,2,128]{3,2,1,0:T(2,128)S(1)} %maximum_add_fusion.2), channel_id=1, source_target_pairs={{0,1},{128,129},{1,0},{129,128},{2,3},{130,131},{3,2},{131,130},{4... | collective-permute-start | bytes 24584 | tf_op jit(solution)/shard_map/totals/ppermute | solution.py:27
  64.3 5.4 %collective-permute-start.19 = (f32[2,4,2,128]{3,2,1,0:T(2,128)S(1)}, f32[2,4,2,128]{3,2,1,0:T(2,128)S(1)}, u32[]{:S(2)}, u32[]{:S(2)}) collective-permute-start(f32[2,4,2,128]{3,2,1,0:T(2,128)S(1)} %maximum_add_fusion.2), channel_id=1, source_target_pairs={{0,128},{128,1},{1,129},{129,0},{2,130},{130,3},{3,131},{131,2},{4... | collective-permute-start | bytes 24584 | tf_op jit(solution)/shard_map/totals/ppermute | solution.py:27
  65.1 4.5 %collective-permute-start.21 = (f32[2,4,2,128]{3,2,1,0:T(2,128)S(1)}, f32[2,4,2,128]{3,2,1,0:T(2,128)S(1)}, u32[]{:S(2)}, u32[]{:S(2)}) collective-permute-start(f32[2,4,2,128]{3,2,1,0:T(2,128)S(1)} %maximum_add_fusion.2), channel_id=1, source_target_pairs={{0,129},{128,0},{1,128},{129,1},{2,131},{130,2},{3,130},{131,3},{4... | collective-permute-start | bytes 24584 | tf_op jit(solution)/shard_map/totals/ppermute | solution.py:27
  67.0 4.1 %collective-permute-start.16 = (f32[2,2,4,128]{3,2,1,0:T(4,128)S(1)}, f32[2,2,4,128]{3,2,1,0:T(4,128)S(1)}, u32[]{:S(2)}, u32[]{:S(2)}) collective-permute-start(f32[2,2,4,128]{3,2,1,0:T(4,128)S(1)} %maximum_add_fusion), channel_id=1, source_target_pairs={{0,32},{16,48},{32,0},{48,16},{1,33},{17,49},{33,1},{49,17},{2,34}... | collective-permute-start | bytes 24584 | tf_op jit(solution)/shard_map/totals/ppermute | solution.py:20
  67.3 3.8 %collective-permute-start.17 = (f32[2,2,4,128]{3,2,1,0:T(4,128)S(1)}, f32[2,2,4,128]{3,2,1,0:T(4,128)S(1)}, u32[]{:S(2)}, u32[]{:S(2)}) collective-permute-start(f32[2,2,4,128]{3,2,1,0:T(4,128)S(1)} %maximum_add_fusion), channel_id=1, source_target_pairs={{0,48},{16,0},{32,16},{48,32},{1,49},{17,1},{33,17},{49,33},{2,50}... | collective-permute-start | bytes 24584 | tf_op jit(solution)/shard_map/totals/ppermute | solution.py:20
  69.6 3.7 %collective-permute-start.15 = (f32[2,2,4,128]{3,2,1,0:T(4,128)S(1)}, f32[2,2,4,128]{3,2,1,0:T(4,128)S(1)}, u32[]{:S(2)}, u32[]{:S(2)}) collective-permute-start(f32[2,2,4,128]{3,2,1,0:T(4,128)S(1)} %maximum_add_fusion), channel_id=1, source_target_pairs={{0,16},{16,32},{32,48},{48,0},{1,17},{17,33},{33,49},{49,1},{2,18}... | collective-permute-start | bytes 24584 | tf_op jit(solution)/shard_map/totals/ppermute | solution.py:20
  76.9 26.7 %collective-permute-start.22 = (f32[4,128,512]{2,1,0:T(8,128)}, f32[4,128,512]{2,1,0:T(8,128)}, u32[]{:S(2)}, u32[]{:S(2)}) collective-permute-start(f32[4,128,512]{2,1,0:T(8,128)} %fusion.68), channel_id=1, source_target_pairs={{0,64},{64,0},{1,65},{65,1},{2,66},{66,2},{3,67},{67,3},{4,68},{68... | collective-permute-start | bytes 3145736 | tf_op jit(solution)/shard_map/pull/ppermute | solution.py:20
  94.1 2.0 %collective-permute-start.29 = (bf16[64,8,512]{2,1,0:T(8,128)(2,1)S(1)}, bf16[64,8,512]{2,1,0:T(8,128)(2,1)S(1)}, u32[]{:S(2)}, u32[]{:S(2)}) collective-permute-start(bf16[64,8,512]{2,1,0:T(8,128)(2,1)S(1)} %fusion.18), channel_id=1, source_target_pairs={{0,64},{64,0},{1,65},{65,1},{2,66},{66,2},{3,67},{67,3},{4,68},{68... | collective-permute-start | bytes 1572872 | tf_op jit(solution)/shard_map/head/ppermute | solution.py:20
  98.3 30.0 %all-to-all-start = ((bf16[64,8,512]{2,1,0:T(8,128)(2,1)}), bf16[64,8,512]{2,1,0:T(8,128)(2,1)S(1)}, u32[]{:S(2)}, u32[]{:S(2)}) async-start(bf16[64,8,512]{2,1,0:T(8,128)(2,1)} %fusion.14), calls=%async_computation | async-start | bytes 1048576 | tf_op jit(solution)/shard_map/head/all_to_all | solution.py:145
  105.2 7.5 %collective-permute-start.23 = (bf16[128,512]{1,0:T(8,128)(2,1)S(1)}, bf16[128,512]{1,0:T(8,128)(2,1)S(1)}, u32[]{:S(2)}, u32[]{:S(2)}) collective-permute-start(bf16[128,512]{1,0:T(8,128)(2,1)S(1)} %get-tuple-element.14), channel_id=1, source_target_pairs={{0,48},{16,0},{32,16},{48,32},{1,49},{17,1},{33,17},{49,33},{2,50}... | collective-permute-start | bytes 393224 | tf_op jit(solution)/shard_map/slopes/ppermute | solution.py:20
  107.7 8.4 %collective-permute-start.24 = (bf16[128,512]{1,0:T(8,128)(2,1)S(1)}, bf16[128,512]{1,0:T(8,128)(2,1)S(1)}, u32[]{:S(2)}, u32[]{:S(2)}) collective-permute-start(bf16[128,512]{1,0:T(8,128)(2,1)S(1)} %get-tuple-element.16), channel_id=1, source_target_pairs={{0,32},{16,48},{32,0},{48,16},{1,33},{17,49},{33,1},{49,17},{2,34}... | collective-permute-start | bytes 393224 | tf_op jit(solution)/shard_map/slopes/ppermute | solution.py:20
  108.1 13.6 %collective-permute-start.25 = (bf16[128,512]{1,0:T(8,128)(2,1)S(1)}, bf16[128,512]{1,0:T(8,128)(2,1)S(1)}, u32[]{:S(2)}, u32[]{:S(2)}) collective-permute-start(bf16[128,512]{1,0:T(8,128)(2,1)S(1)} %get-tuple-element.15), channel_id=1, source_target_pairs={{0,16},{16,32},{32,48},{48,0},{1,17},{17,33},{33,49},{49,1},{2,18}... | collective-permute-start | bytes 393224 | tf_op jit(solution)/shard_map/slopes/ppermute | solution.py:20
  122.0 7.2 %collective-permute-start.26 = (bf16[32,512]{1,0:T(8,128)(2,1)S(1)}, bf16[32,512]{1,0:T(8,128)(2,1)S(1)}, u32[]{:S(2)}, u32[]{:S(2)}) collective-permute-start(bf16[32,512]{1,0:T(8,128)(2,1)S(1)} %get-tuple-element.26), channel_id=1, source_target_pairs={{0,12},{4,0},{8,4},{12,8},{1,13},{5,1},{9,5},{13,9},{2,14},{6,2},{... | collective-permute-start | bytes 98312 | tf_op jit(solution)/shard_map/route_back/ppermute | solution.py:20
  124.9 6.8 %collective-permute-start.27 = (bf16[32,512]{1,0:T(8,128)(2,1)S(1)}, bf16[32,512]{1,0:T(8,128)(2,1)S(1)}, u32[]{:S(2)}, u32[]{:S(2)}) collective-permute-start(bf16[32,512]{1,0:T(8,128)(2,1)S(1)} %get-tuple-element.25), channel_id=1, source_target_pairs={{0,8},{4,12},{8,0},{12,4},{1,9},{5,13},{9,1},{13,5},{2,10},{6,14},... | collective-permute-start | bytes 98312 | tf_op jit(solution)/shard_map/route_back/ppermute | solution.py:20
  126.4 5.3 %collective-permute-start.28 = (bf16[32,512]{1,0:T(8,128)(2,1)S(1)}, bf16[32,512]{1,0:T(8,128)(2,1)S(1)}, u32[]{:S(2)}, u32[]{:S(2)}) collective-permute-start(bf16[32,512]{1,0:T(8,128)(2,1)S(1)} %get-tuple-element.24), channel_id=1, source_target_pairs={{0,4},{4,8},{8,12},{12,0},{1,5},{5,9},{9,13},{13,1},{2,6},{6,10},{... | collective-permute-start | bytes 98312 | tf_op jit(solution)/shard_map/route_back/ppermute | solution.py:20
  128.4 4.6 %collective-permute-start.30 = (f32[8,512]{1,0:T(8,128)S(1)}, f32[8,512]{1,0:T(8,128)S(1)}, u32[]{:S(2)}, u32[]{:S(2)}) collective-permute-start(f32[8,512]{1,0:T(8,128)S(1)} %convert_reduce_fusion), channel_id=1, source_target_pairs={{0,128},{128,0},{1,129},{129,1},{2,130},{130,2},{3,131},{131,3},{4... | collective-permute-start | bytes 49160 | tf_op jit(solution)/shard_map/head/ppermute | solution.py:20
  (8 other events, 56.2 us)
where the time goes:
time: 138 us; the launch traced here: 137 us
  starting transfers between devices  60.9 us (44%)
  waiting for transfers between devices  35.1 us (25%)
  other arithmetic  15.6 us (11%)
  matrix products  11.6 us (8%)
  local copies, waits for them, and re-layouts  9.25 us (7%)
  blocking collectives  3.59 us (3%)
    ppermute x25, starting transfers between devices, shift(): lax.ppermute(value, axis, [(i, (i + distance) % size) for i in range(size)])  45.5 us
    ppermute x25, waiting for transfers between devices, shift(): lax.ppermute(value, axis, [(i, (i + distance) % size) for i in range(size)])  31.4 us
    ppermute x6, starting transfers between devices, shift_y(): lax.ppermute(value, ('yl', 'yh'), [(seat[y], seat[(y + distance) % 4]) fo...  10 us
    all_to_all x1, starting transfers between devices, body(): spread = lax.all_to_all(part, KEY, split_axis=0, concat_axis=0, tiled=True)  5.33 us
    unnamed x27, local copies, waits for them, and re-layouts  4.58 us
    ppermute x6, waiting for transfers between devices, shift_y(): lax.ppermute(value, ('yl', 'yh'), [(seat[y], seat[(y + distance) % 4]) fo...  3.67 us
    all_gather x1, blocking collectives, body(): grad_head = lax.all_gather(piece, 'c', axis=0, tiled=True)  3.59 us
    dot_general x1, matrix products, body(): lax.dot_general(rows_a, slopes_part, (((0,), (0,)), ((), ())), preferred_...  2.93 us
  transfers between devices with their start and end apart: 32, of which 13 were waited for; matrix products, arithmetic and copies ran while one was open for 13% of the time, Pallas kernels for 0%

commit v1 on v0

--- a/solution.py
+++ b/solution.py
@@ -145,7 +145,9 @@
         spread = lax.all_to_all(part, KEY, split_axis=0, concat_axis=0, tiled=True)
         piece = jnp.sum(spread.astype(f32), axis=0)
         piece = piece + shift(piece, "yl", 2, 1)
-        grad_head = lax.all_gather(piece, "c", axis=0, tiled=True)
+        grad_head = jnp.concatenate(
+            lax.all_to_all(jnp.stack([piece] * lax.axis_size("c")), "c", 0, 0), axis=0
+        )
     with jax.named_scope("slopes"):
         pull = pull_near + crossing
         parts = [shift(pull[d].astype(bf16), "x", 4, -d).astype(f32) for d in range(1, 4)]

time: 138 us -> 140 us (1.014)
  blocking collectives: 3.59 us -> 5.51 us
    all_to_all x0 -> x1, blocking collectives: none -> 5.51 us  [body(): lax.all_to_all(jnp.stack([piece] * lax.axis_size('c')), 'c', 0, 0)]
    all_gather x1 -> x0, blocking collectives: 3.59 us -> none  [body(): grad_head = lax.all_gather(piece, 'c', axis=0, tiled=True)]
where the time goes in v1:
time: 140 us; the launch traced here: 139 us
  starting transfers between devices  60.9 us (44%)
  waiting for transfers between devices  35.1 us (25%)
  other arithmetic  15.6 us (11%)
  matrix products  11.6 us (8%)
  local copies, waits for them, and re-layouts  9.25 us (7%)
  blocking collectives  5.51 us (4%)
    ppermute x25, starting transfers between devices, shift(): lax.ppermute(value, axis, [(i, (i + distance) % size) for i in range(size)])  45.5 us
    ppermute x25, waiting for transfers between devices, shift(): lax.ppermute(value, axis, [(i, (i + distance) % size) for i in range(size)])  31.4 us
    ppermute x6, starting transfers between devices, shift_y(): lax.ppermute(value, ('yl', 'yh'), [(seat[y], seat[(y + distance) % 4]) fo...  10 us
    all_to_all x1, blocking collectives, body(): lax.all_to_all(jnp.stack([piece] * lax.axis_size('c')), 'c', 0, 0)  5.51 us
    all_to_all x1, starting transfers between devices, body(): spread = lax.all_to_all(part, KEY, split_axis=0, concat_axis=0, tiled=True)  5.33 us
    unnamed x27, local copies, waits for them, and re-layouts  4.58 us
    ppermute x6, waiting for transfers between devices, shift_y(): lax.ppermute(value, ('yl', 'yh'), [(seat[y], seat[(y + distance) % 4]) fo...  3.67 us
    dot_general x1, matrix products, body(): lax.dot_general(rows_a, slopes_part, (((0,), (0,)), ((), ())), preferred_...  2.93 us
  transfers between devices with their start and end apart: 32, of which 13 were waited for; matrix products, arithmetic and copies ran while one was open for 13% of the time, Pallas kernels for 0%

profile of v1, /device:TPU:1, one launch (start us, length us, event | category | flops | bytes accessed | tf_op | source)
XLA Modules:
  0.0 139.2 jit_solution(8948073103308956055)
XLA Ops:
  3.5 3.9 %collective-permute-start = (bf16[32,1152]{1,0:T(8,128)(2,1)S(1)}, bf16[32,1152]{1,0:T(8,128)(2,1)S(1)}, u32[]{:S(2)}, u32[]{:S(2)}) collective-permute-start(bf16[32,1152]{1,0:T(8,128)(2,1)S(1)} %get-tuple-element.22), channel_id=1, source_target_pairs={{0,4},{4,8},{8,12},{12,0},{1,5},{5,9},{9,13},{13,1},{2,6},{6,10},{... | collective-permute-start | bytes 221192 | tf_op jit(solution)/shard_map/route_out/ppermute | solution.py:20
  7.4 5.1 %collective-permute-start.1 = (bf16[32,1152]{1,0:T(8,128)(2,1)S(1)}, bf16[32,1152]{1,0:T(8,128)(2,1)S(1)}, u32[]{:S(2)}, u32[]{:S(2)}) collective-permute-start(bf16[32,1152]{1,0:T(8,128)(2,1)S(1)} %get-tuple-element.21), channel_id=1, source_target_pairs={{0,8},{4,12},{8,0},{12,4},{1,9},{5,13},{9,1},{13,5},{2,10},{6,14},... | collective-permute-start | bytes 221192 | tf_op jit(solution)/shard_map/route_out/ppermute | solution.py:20
  12.6 2.4 %collective-permute-start.2 = (bf16[32,1152]{1,0:T(8,128)(2,1)S(1)}, bf16[32,1152]{1,0:T(8,128)(2,1)S(1)}, u32[]{:S(2)}, u32[]{:S(2)}) collective-permute-start(bf16[32,1152]{1,0:T(8,128)(2,1)S(1)} %get-tuple-element.20), channel_id=1, source_target_pairs={{0,12},{4,0},{8,4},{12,8},{1,13},{5,1},{9,5},{13,9},{2,14},{6,2},{... | collective-permute-start | bytes 221192 | tf_op jit(solution)/shard_map/route_out/ppermute | solution.py:20
  14.9 2.0 %collective-permute-done.1 = bf16[32,1152]{1,0:T(8,128)(2,1)S(1)} collective-permute-done((bf16[32,1152]{1,0:T(8,128)(2,1)S(1)}, bf16[32,1152]{1,0:T(8,128)(2,1)S(1)}, u32[]{:S(2)}, u32[]{:S(2)}) %collective-permute-start.1) | collective-permute-done | bytes 73760 | tf_op jit(solution)/shard_map/route_out/ppermute | solution.py:20
  16.9 3.9 %collective-permute-done.2 = bf16[32,1152]{1,0:T(8,128)(2,1)S(1)} collective-permute-done((bf16[32,1152]{1,0:T(8,128)(2,1)S(1)}, bf16[32,1152]{1,0:T(8,128)(2,1)S(1)}, u32[]{:S(2)}, u32[]{:S(2)}) %collective-permute-start.2) | collective-permute-done | bytes 73760 | tf_op jit(solution)/shard_map/route_out/ppermute | solution.py:20
  22.2 2.5 %collective-permute-start.4 = (bf16[128,1152]{1,0:T(8,128)(2,1)S(1)}, bf16[128,1152]{1,0:T(8,128)(2,1)S(1)}, u32[]{:S(2)}, u32[]{:S(2)}) collective-permute-start(bf16[128,1152]{1,0:T(8,128)(2,1)S(1)} %get-tuple-element.18), channel_id=1, source_target_pairs={{0,32},{16,48},{32,0},{48,16},{1,33},{17,49},{33,1},{49,17},{2,34}... | collective-permute-start | bytes 884744 | tf_op jit(solution)/shard_map/gather_sets/ppermute | solution.py:20
  28.1 2.9 %collective-permute-done.7 = bf16[144,512]{1,0:T(8,128)(2,1)S(1)} collective-permute-done((bf16[144,512]{1,0:T(8,128)(2,1)S(1)}, bf16[144,512]{1,0:T(8,128)(2,1)S(1)}, u32[]{:S(2)}, u32[]{:S(2)}) %collective-permute-start.7) | collective-permute-done | bytes 147488 | tf_op jit(solution)/shard_map/gather_sets/ppermute | solution.py:20
  30.9 2.9 %collective-permute-start.10 = (bf16[144,512]{1,0:T(8,128)(2,1)S(1)}, bf16[144,512]{1,0:T(8,128)(2,1)S(1)}, u32[]{:S(2)}, u32[]{:S(2)}) collective-permute-start(bf16[144,512]{1,0:T(8,128)(2,1)S(1)} %pad_maximum_fusion.2), channel_id=1, source_target_pairs={{0,1},{128,129},{1,0},{129,128},{2,3},{130,131},{3,2},{131,130},{4... | collective-permute-start | bytes 442376 | tf_op jit(solution)/shard_map/gather_sets/ppermute | solution.py:27
  34.7 2.1 %collective-permute-done.10 = bf16[144,512]{1,0:T(8,128)(2,1)S(1)} collective-permute-done((bf16[144,512]{1,0:T(8,128)(2,1)S(1)}, bf16[144,512]{1,0:T(8,128)(2,1)S(1)}, u32[]{:S(2)}, u32[]{:S(2)}) %collective-permute-start.10) | collective-permute-done | bytes 147488 | tf_op jit(solution)/shard_map/gather_sets/ppermute | solution.py:27
  40.7 3.9 %collective-permute-start.6 = (bf16[4,128,1152]{2,1,0:T(8,128)(2,1)S(1)}, bf16[4,128,1152]{2,1,0:T(8,128)(2,1)S(1)}, u32[]{:S(2)}, u32[]{:S(2)}) collective-permute-start(bf16[4,128,1152]{2,1,0:T(8,128)(2,1)S(1)} %pad_maximum_fusion), channel_id=1, source_target_pairs={{0,64},{64,0},{1,65},{65,1},{2,66},{66,2},{3,67},{67,3},{4,68},{68... | collective-permute-start | bytes 3538952 | tf_op jit(solution)/shard_map/gather_sets/ppermute | solution.py:20
  44.8 2.1 %collective-permute-done.13 = bf16[144,512]{1,0:T(8,128)(2,1)S(1)} collective-permute-done((bf16[144,512]{1,0:T(8,128)(2,1)S(1)}, bf16[144,512]{1,0:T(8,128)(2,1)S(1)}, u32[]{:S(2)}, u32[]{:S(2)}) %collective-permute-start.13) | collective-permute-done | bytes 147488 | tf_op jit(solution)/shard_map/gather_sets/ppermute | solution.py:20
  53.1 2.2 %fusion.9 = (f32[1024]{0:T(1024)S(1)}, f32[1024]{0:T(1024)S(1)}) fusion(pred[1024]{0:T(1024)(128)(4,1)S(1)} %iota_compare_fusion.5, s32[1024]{0:T(1024)S(1)} %bitcast.113, s32[1024]{0:T(1024)S(1)} %bitcast.115), kind=kLoop, calls=%fused_computation.20 | loop fusion | flops 8386560 | bytes 17408 | tf_op jit(solution)/shard_map/scores/reduce_sum | solution.py:97
  56.6 1.9 %fusion.58 = (f32[1024]{0:T(1024)S(1)}, f32[1024]{0:T(1024)S(1)}, f32[1024,1024]{1,0:T(8,128)S(1)}) fusion(bf16[1024,512]{1,0:T(8,128)(2,1)S(1)} %bitcast.93, f32[1024,512]{0,1:T(8,128)S(1)} %get-tuple-element.48, f32[1024]{0:T(1024)S(1)} %add_sqrt_fusion, pred[1024]{0:T(1024)(128)(4,1)S(1)} %iota_compare_fusion.5), kind=kOutput, calls=%fused_computation.126 | convolution fusion | flops 1081079808 | bytes 7353344 | tf_op jit(solution)/shard_map/scores/dot_general | solution.py:86
  58.6 3.4 %collective-permute-start.14 = (f32[2,2,4,128]{3,2,1,0:T(4,128)S(1)}, f32[2,2,4,128]{3,2,1,0:T(4,128)S(1)}, u32[]{:S(2)}, u32[]{:S(2)}) collective-permute-start(f32[2,2,4,128]{3,2,1,0:T(4,128)S(1)} %pad_maximum_fusion.4), channel_id=1, source_target_pairs={{0,64},{64,0},{1,65},{65,1},{2,66},{66,2},{3,67},{67,3},{4,68},{68... | collective-permute-start | bytes 24584 | tf_op jit(solution)/shard_map/totals/ppermute | solution.py:20
  62.1 2.2 %collective-permute-start.20 = (f32[2,4,2,128]{3,2,1,0:T(2,128)S(1)}, f32[2,4,2,128]{3,2,1,0:T(2,128)S(1)}, u32[]{:S(2)}, u32[]{:S(2)}) collective-permute-start(f32[2,4,2,128]{3,2,1,0:T(2,128)S(1)} %maximum_add_fusion.2), channel_id=1, source_target_pairs={{0,1},{128,129},{1,0},{129,128},{2,3},{130,131},{3,2},{131,130},{4... | collective-permute-start | bytes 24584 | tf_op jit(solution)/shard_map/totals/ppermute | solution.py:27
  67.3 2.3 %collective-permute-start.17 = (f32[2,2,4,128]{3,2,1,0:T(4,128)S(1)}, f32[2,2,4,128]{3,2,1,0:T(4,128)S(1)}, u32[]{:S(2)}, u32[]{:S(2)}) collective-permute-start(f32[2,2,4,128]{3,2,1,0:T(4,128)S(1)} %maximum_add_fusion), channel_id=1, source_target_pairs={{0,48},{16,0},{32,16},{48,32},{1,49},{17,1},{33,17},{49,33},{2,50}... | collective-permute-start | bytes 24584 | tf_op jit(solution)/shard_map/totals/ppermute | solution.py:20
  71.1 2.2 %collective-permute-done.15 = f32[2,2,4,128]{3,2,1,0:T(4,128)S(1)} collective-permute-done((f32[2,2,4,128]{3,2,1,0:T(4,128)S(1)}, f32[2,2,4,128]{3,2,1,0:T(4,128)S(1)}, u32[]{:S(2)}, u32[]{:S(2)}) %collective-permute-start.15) | collective-permute-done | bytes 8224 | tf_op jit(solution)/shard_map/totals/ppermute | solution.py:20
  76.9 5.8 %collective-permute-start.22 = (f32[4,128,512]{2,1,0:T(8,128)}, f32[4,128,512]{2,1,0:T(8,128)}, u32[]{:S(2)}, u32[]{:S(2)}) collective-permute-start(f32[4,128,512]{2,1,0:T(8,128)} %fusion.68), channel_id=1, source_target_pairs={{0,64},{64,0},{1,65},{65,1},{2,66},{66,2},{3,67},{67,3},{4,68},{68... | collective-permute-start | bytes 3145736 | tf_op jit(solution)/shard_map/pull/ppermute | solution.py:20
  82.7 2.8 %maximum_multiply_fusion = f32[8,128,512]{2,1,0:T(8,128)} fusion(f32[4,128,512]{2,1,0:T(8,128)} %fusion.68, f32[4,128,512]{2,1,0:T(8,128)S(1)} %fusion.67), kind=kLoop, calls=%fused_computation.15 | loop fusion | flops 1048576 | bytes 4194304 | tf_op jit(solution)/shard_map/head/div | solution.py:136
  85.6 1.9 %copy.10 = f32[1024,512]{0,1:T(8,128)S(1)} copy(f32[1024,512]{1,0:T(8,128)} %bitcast.85) | data formatting | bytes 4194304 | tf_op jit(solution)/shard_map/head/div | solution.py:136
  87.5 2.0 %multiply_reduce_fusion = f32[1024]{0:T(1024)S(1)} fusion(f32[1024,512]{0,1:T(8,128)S(1)} %copy.10, f32[1024,512]{0,1:T(8,128)} %copy-done.3, f32[1024]{0:T(1024)S(1)} %add_sqrt_fusion), kind=kLoop, calls=%fused_computation.17 | loop fusion | flops 1571840 | bytes 4202496 | tf_op jit(solution)/shard_map/head/reduce_sum | solution.py:131
  89.7 2.9 %fusion.10 = f32[1024,512]{1,0:T(8,128)S(1)} fusion(bf16[1024,1152]{1,0:T(8,128)(2,1)} %bitcast.98, f32[1024,512]{0,1:T(8,128)S(1)} %copy.10, f32[1024]{0:T(1024)S(1)} %multiply_reduce_fusion, f32[1024]{0:T(1024)S(1)} %add_sqrt_fusion, f32[1024,512]{0,1:T(8,128)S(1)} %copy-done.4), kind=kOutput, calls=%fused_computation.21 | convolution fusion | flops 1076363264 | bytes 8396800 | tf_op jit(solution)/shard_map/head/dot_general | solution.py:137
  96.1 2.2 %fusion.14 = bf16[64,8,512]{2,1,0:T(8,128)(2,1)} fusion(bf16[64,8,512]{2,1,0:T(8,128)(2,1)S(1)} %collective-permute-done.29, f32[64,2,8,512]{3,2,1,0:T(8,128)} %bitcast.90, s32[]{:T(128)S(6)} %select_n.40), kind=kLoop, calls=%fused_computation.29 | loop fusion | flops 786432 | bytes 2097156 | tf_op jit(solution)/shard_map/head/convert_element_type | solution.py:144
  98.3 5.3 %all-to-all-start = ((bf16[64,8,512]{2,1,0:T(8,128)(2,1)}), bf16[64,8,512]{2,1,0:T(8,128)(2,1)S(1)}, u32[]{:S(2)}, u32[]{:S(2)}) async-start(bf16[64,8,512]{2,1,0:T(8,128)(2,1)} %fusion.14), calls=%async_computation | async-start | bytes 1048576 | tf_op jit(solution)/shard_map/head/all_to_all | solution.py:145
  105.2 2.5 %collective-permute-start.23 = (bf16[128,512]{1,0:T(8,128)(2,1)S(1)}, bf16[128,512]{1,0:T(8,128)(2,1)S(1)}, u32[]{:S(2)}, u32[]{:S(2)}) collective-permute-start(bf16[128,512]{1,0:T(8,128)(2,1)S(1)} %get-tuple-element.14), channel_id=1, source_target_pairs={{0,48},{16,0},{32,16},{48,32},{1,49},{17,1},{33,17},{49,33},{2,50}... | collective-permute-start | bytes 393224 | tf_op jit(solution)/shard_map/slopes/ppermute | solution.py:20
  108.7 4.0 %collective-permute-done.23 = bf16[128,512]{1,0:T(8,128)(2,1)S(1)} collective-permute-done((bf16[128,512]{1,0:T(8,128)(2,1)S(1)}, bf16[128,512]{1,0:T(8,128)(2,1)S(1)}, u32[]{:S(2)}, u32[]{:S(2)}) %collective-permute-start.23) | collective-permute-done | bytes 131104 | tf_op jit(solution)/shard_map/slopes/ppermute | solution.py:20
  112.7 3.4 %collective-permute-done.24 = bf16[128,512]{1,0:T(8,128)(2,1)S(1)} collective-permute-done((bf16[128,512]{1,0:T(8,128)(2,1)S(1)}, bf16[128,512]{1,0:T(8,128)(2,1)S(1)}, u32[]{:S(2)}, u32[]{:S(2)}) %collective-permute-start.24) | collective-permute-done | bytes 131104 | tf_op jit(solution)/shard_map/slopes/ppermute | solution.py:20
  116.1 5.6 %collective-permute-done.25 = bf16[128,512]{1,0:T(8,128)(2,1)S(1)} collective-permute-done((bf16[128,512]{1,0:T(8,128)(2,1)S(1)}, bf16[128,512]{1,0:T(8,128)(2,1)S(1)}, u32[]{:S(2)}, u32[]{:S(2)}) %collective-permute-start.25) | collective-permute-done | bytes 131104 | tf_op jit(solution)/shard_map/slopes/ppermute | solution.py:20
  122.0 2.9 %collective-permute-start.26 = (bf16[32,512]{1,0:T(8,128)(2,1)S(1)}, bf16[32,512]{1,0:T(8,128)(2,1)S(1)}, u32[]{:S(2)}, u32[]{:S(2)}) collective-permute-start(bf16[32,512]{1,0:T(8,128)(2,1)S(1)} %get-tuple-element.26), channel_id=1, source_target_pairs={{0,12},{4,0},{8,4},{12,8},{1,13},{5,1},{9,5},{13,9},{2,14},{6,2},{... | collective-permute-start | bytes 98312 | tf_op jit(solution)/shard_map/route_back/ppermute | solution.py:20
  126.4 1.9 %collective-permute-start.28 = (bf16[32,512]{1,0:T(8,128)(2,1)S(1)}, bf16[32,512]{1,0:T(8,128)(2,1)S(1)}, u32[]{:S(2)}, u32[]{:S(2)}) collective-permute-start(bf16[32,512]{1,0:T(8,128)(2,1)S(1)} %get-tuple-element.24), channel_id=1, source_target_pairs={{0,4},{4,8},{8,12},{12,0},{1,5},{5,9},{9,13},{13,1},{2,6},{6,10},{... | collective-permute-start | bytes 98312 | tf_op jit(solution)/shard_map/route_back/ppermute | solution.py:20
  129.2 2.4 %collective-permute-done.27 = bf16[32,512]{1,0:T(8,128)(2,1)S(1)} collective-permute-done((bf16[32,512]{1,0:T(8,128)(2,1)S(1)}, bf16[32,512]{1,0:T(8,128)(2,1)S(1)}, u32[]{:S(2)}, u32[]{:S(2)}) %collective-permute-start.27) | collective-permute-done | bytes 32800 | tf_op jit(solution)/shard_map/route_back/ppermute | solution.py:20
  133.0 5.5 %all_to_all.10 = f32[2,8,512]{2,1,0:T(8,128)S(1)} all-to-all(f32[2,8,512]{2,1,0:T(8,128)S(1)} %pad_maximum_fusion.3), channel_id=1, replica_groups=mesh['yl'=2,'c'=2,'x'=4,'zh'=4,'zl'=2,'yh'=2] {'c'}, dimensions={0} | all-to-all | bytes 65536 | tf_op jit(solution)/shard_map/head/all_to_all | solution.py:149
  (131 shorter events, 38.7 us)
Async XLA Ops:
  3.5 11.4 %collective-permute-start = (bf16[32,1152]{1,0:T(8,128)(2,1)S(1)}, bf16[32,1152]{1,0:T(8,128)(2,1)S(1)}, u32[]{:S(2)}, u32[]{:S(2)}) collective-permute-start(bf16[32,1152]{1,0:T(8,128)(2,1)S(1)} %get-tuple-element.22), channel_id=1, source_target_pairs={{0,4},{4,8},{8,12},{12,0},{1,5},{5,9},{9,13},{13,1},{2,6},{6,10},{... | collective-permute-start | bytes 221192 | tf_op jit(solution)/shard_map/route_out/ppermute | solution.py:20
  7.4 9.5 %collective-permute-start.1 = (bf16[32,1152]{1,0:T(8,128)(2,1)S(1)}, bf16[32,1152]{1,0:T(8,128)(2,1)S(1)}, u32[]{:S(2)}, u32[]{:S(2)}) collective-permute-start(bf16[32,1152]{1,0:T(8,128)(2,1)S(1)} %get-tuple-element.21), channel_id=1, source_target_pairs={{0,8},{4,12},{8,0},{12,4},{1,9},{5,13},{9,1},{13,5},{2,10},{6,14},... | collective-permute-start | bytes 221192 | tf_op jit(solution)/shard_map/route_out/ppermute | solution.py:20
  12.6 8.3 %collective-permute-start.2 = (bf16[32,1152]{1,0:T(8,128)(2,1)S(1)}, bf16[32,1152]{1,0:T(8,128)(2,1)S(1)}, u32[]{:S(2)}, u32[]{:S(2)}) collective-permute-start(bf16[32,1152]{1,0:T(8,128)(2,1)S(1)} %get-tuple-element.20), channel_id=1, source_target_pairs={{0,12},{4,0},{8,4},{12,8},{1,13},{5,1},{9,5},{13,9},{2,14},{6,2},{... | collective-permute-start | bytes 221192 | tf_op jit(solution)/shard_map/route_out/ppermute | solution.py:20
  20.9 18.2 %collective-permute-start.3 = (bf16[128,1152]{1,0:T(8,128)(2,1)S(1)}, bf16[128,1152]{1,0:T(8,128)(2,1)S(1)}, u32[]{:S(2)}, u32[]{:S(2)}) collective-permute-start(bf16[128,1152]{1,0:T(8,128)(2,1)S(1)} %get-tuple-element.18), channel_id=1, source_target_pairs={{0,16},{16,32},{32,48},{48,0},{1,17},{17,33},{33,49},{49,1},{2,18}... | collective-permute-start | bytes 884744 | tf_op jit(solution)/shard_map/gather_sets/ppermute | solution.py:20
  22.2 18.4 %collective-permute-start.4 = (bf16[128,1152]{1,0:T(8,128)(2,1)S(1)}, bf16[128,1152]{1,0:T(8,128)(2,1)S(1)}, u32[]{:S(2)}, u32[]{:S(2)}) collective-permute-start(bf16[128,1152]{1,0:T(8,128)(2,1)S(1)} %get-tuple-element.18), channel_id=1, source_target_pairs={{0,32},{16,48},{32,0},{48,16},{1,33},{17,49},{33,1},{49,17},{2,34}... | collective-permute-start | bytes 884744 | tf_op jit(solution)/shard_map/gather_sets/ppermute | solution.py:20
  24.6 15.9 %collective-permute-start.5 = (bf16[128,1152]{1,0:T(8,128)(2,1)S(1)}, bf16[128,1152]{1,0:T(8,128)(2,1)S(1)}, u32[]{:S(2)}, u32[]{:S(2)}) collective-permute-start(bf16[128,1152]{1,0:T(8,128)(2,1)S(1)} %get-tuple-element.18), channel_id=1, source_target_pairs={{0,48},{16,0},{32,16},{48,32},{1,49},{17,1},{33,17},{49,33},{2,50}... | collective-permute-start | bytes 884744 | tf_op jit(solution)/shard_map/gather_sets/ppermute | solution.py:20
  26.5 4.4 %collective-permute-start.7 = (bf16[144,512]{1,0:T(8,128)(2,1)S(1)}, bf16[144,512]{1,0:T(8,128)(2,1)S(1)}, u32[]{:S(2)}, u32[]{:S(2)}) collective-permute-start(bf16[144,512]{1,0:T(8,128)(2,1)S(1)} %pad_maximum_fusion.2), channel_id=1, source_target_pairs={{0,2},{2,0},{1,3},{3,1},{4,6},{6,4},{5,7},{7,5},{8,10},{10,8},{9,1... | collective-permute-start | bytes 442376 | tf_op jit(solution)/shard_map/gather_sets/ppermute | solution.py:20
  26.6 7.2 %collective-permute-start.8 = (bf16[144,512]{1,0:T(8,128)(2,1)S(1)}, bf16[144,512]{1,0:T(8,128)(2,1)S(1)}, u32[]{:S(2)}, u32[]{:S(2)}) collective-permute-start(bf16[144,512]{1,0:T(8,128)(2,1)S(1)} %pad_maximum_fusion.2), channel_id=1, source_target_pairs={{0,128},{128,1},{1,129},{129,0},{2,130},{130,3},{3,131},{131,2},{4... | collective-permute-start | bytes 442376 | tf_op jit(solution)/shard_map/gather_sets/ppermute | solution.py:27
  30.9 5.9 %collective-permute-start.10 = (bf16[144,512]{1,0:T(8,128)(2,1)S(1)}, bf16[144,512]{1,0:T(8,128)(2,1)S(1)}, u32[]{:S(2)}, u32[]{:S(2)}) collective-permute-start(bf16[144,512]{1,0:T(8,128)(2,1)S(1)} %pad_maximum_fusion.2), channel_id=1, source_target_pairs={{0,1},{128,129},{1,0},{129,128},{2,3},{130,131},{3,2},{131,130},{4... | collective-permute-start | bytes 442376 | tf_op jit(solution)/shard_map/gather_sets/ppermute | solution.py:27
  33.9 5.2 %collective-permute-start.12 = (bf16[144,512]{1,0:T(8,128)(2,1)S(1)}, bf16[144,512]{1,0:T(8,128)(2,1)S(1)}, u32[]{:S(2)}, u32[]{:S(2)}) collective-permute-start(bf16[144,512]{1,0:T(8,128)(2,1)S(1)} %pad_maximum_fusion.2), channel_id=1, source_target_pairs={{0,129},{128,0},{1,128},{129,1},{2,131},{130,2},{3,130},{131,3},{4... | collective-permute-start | bytes 442376 | tf_op jit(solution)/shard_map/gather_sets/ppermute | solution.py:27
  36.8 7.9 %collective-permute-start.9 = (bf16[144,512]{1,0:T(8,128)(2,1)S(1)}, bf16[144,512]{1,0:T(8,128)(2,1)S(1)}, u32[]{:S(2)}, u32[]{:S(2)}) collective-permute-start(bf16[144,512]{1,0:T(8,128)(2,1)S(1)} %collective-permute-done.8), channel_id=1, source_target_pairs={{0,2},{2,0},{1,3},{3,1},{4,6},{6,4},{5,7},{7,5},{8,10},{10,8},{9,1... | collective-permute-start | bytes 442376 | tf_op jit(solution)/shard_map/gather_sets/ppermute | solution.py:20
  39.1 5.7 %collective-permute-start.11 = (bf16[144,512]{1,0:T(8,128)(2,1)S(1)}, bf16[144,512]{1,0:T(8,128)(2,1)S(1)}, u32[]{:S(2)}, u32[]{:S(2)}) collective-permute-start(bf16[144,512]{1,0:T(8,128)(2,1)S(1)} %collective-permute-done.10), channel_id=1, source_target_pairs={{0,2},{2,0},{1,3},{3,1},{4,6},{6,4},{5,7},{7,5},{8,10},{10,8},{9,1... | collective-permute-start | bytes 442376 | tf_op jit(solution)/shard_map/gather_sets/ppermute | solution.py:20
  39.1 7.9 %collective-permute-start.13 = (bf16[144,512]{1,0:T(8,128)(2,1)S(1)}, bf16[144,512]{1,0:T(8,128)(2,1)S(1)}, u32[]{:S(2)}, u32[]{:S(2)}) collective-permute-start(bf16[144,512]{1,0:T(8,128)(2,1)S(1)} %collective-permute-done.12), channel_id=1, source_target_pairs={{0,2},{2,0},{1,3},{3,1},{4,6},{6,4},{5,7},{7,5},{8,10},{10,8},{9,1... | collective-permute-start | bytes 442376 | tf_op jit(solution)/shard_map/gather_sets/ppermute | solution.py:20
  40.7 7.4 %collective-permute-start.6 = (bf16[4,128,1152]{2,1,0:T(8,128)(2,1)S(1)}, bf16[4,128,1152]{2,1,0:T(8,128)(2,1)S(1)}, u32[]{:S(2)}, u32[]{:S(2)}) collective-permute-start(bf16[4,128,1152]{2,1,0:T(8,128)(2,1)S(1)} %pad_maximum_fusion), channel_id=1, source_target_pairs={{0,64},{64,0},{1,65},{65,1},{2,66},{66,2},{3,67},{67,3},{4,68},{68... | collective-permute-start | bytes 3538952 | tf_op jit(solution)/shard_map/gather_sets/ppermute | solution.py:20
  58.5 3.5 %collective-permute-start.18 = (f32[2,4,2,128]{3,2,1,0:T(2,128)S(1)}, f32[2,4,2,128]{3,2,1,0:T(2,128)S(1)}, u32[]{:S(2)}, u32[]{:S(2)}) collective-permute-start(f32[2,4,2,128]{3,2,1,0:T(2,128)S(1)} %pad_maximum_fusion.5), channel_id=1, source_target_pairs={{0,2},{2,0},{1,3},{3,1},{4,6},{6,4},{5,7},{7,5},{8,10},{10,8},{9,1... | collective-permute-start | bytes 24584 | tf_op jit(solution)/shard_map/totals/ppermute | solution.py:20
  58.6 8.3 %collective-permute-start.14 = (f32[2,2,4,128]{3,2,1,0:T(4,128)S(1)}, f32[2,2,4,128]{3,2,1,0:T(4,128)S(1)}, u32[]{:S(2)}, u32[]{:S(2)}) collective-permute-start(f32[2,2,4,128]{3,2,1,0:T(4,128)S(1)} %pad_maximum_fusion.4), channel_id=1, source_target_pairs={{0,64},{64,0},{1,65},{65,1},{2,66},{66,2},{3,67},{67,3},{4,68},{68... | collective-permute-start | bytes 24584 | tf_op jit(solution)/shard_map/totals/ppermute | solution.py:20
  62.1 7.6 %collective-permute-start.20 = (f32[2,4,2,128]{3,2,1,0:T(2,128)S(1)}, f32[2,4,2,128]{3,2,1,0:T(2,128)S(1)}, u32[]{:S(2)}, u32[]{:S(2)}) collective-permute-start(f32[2,4,2,128]{3,2,1,0:T(2,128)S(1)} %maximum_add_fusion.2), channel_id=1, source_target_pairs={{0,1},{128,129},{1,0},{129,128},{2,3},{130,131},{3,2},{131,130},{4... | collective-permute-start | bytes 24584 | tf_op jit(solution)/shard_map/totals/ppermute | solution.py:27
  64.3 5.4 %collective-permute-start.19 = (f32[2,4,2,128]{3,2,1,0:T(2,128)S(1)}, f32[2,4,2,128]{3,2,1,0:T(2,128)S(1)}, u32[]{:S(2)}, u32[]{:S(2)}) collective-permute-start(f32[2,4,2,128]{3,2,1,0:T(2,128)S(1)} %maximum_add_fusion.2), channel_id=1, source_target_pairs={{0,128},{128,1},{1,129},{129,0},{2,130},{130,3},{3,131},{131,2},{4... | collective-permute-start | bytes 24584 | tf_op jit(solution)/shard_map/totals/ppermute | solution.py:27
  65.1 4.5 %collective-permute-start.21 = (f32[2,4,2,128]{3,2,1,0:T(2,128)S(1)}, f32[2,4,2,128]{3,2,1,0:T(2,128)S(1)}, u32[]{:S(2)}, u32[]{:S(2)}) collective-permute-start(f32[2,4,2,128]{3,2,1,0:T(2,128)S(1)} %maximum_add_fusion.2), channel_id=1, source_target_pairs={{0,129},{128,0},{1,128},{129,1},{2,131},{130,2},{3,130},{131,3},{4... | collective-permute-start | bytes 24584 | tf_op jit(solution)/shard_map/totals/ppermute | solution.py:27
  67.0 4.1 %collective-permute-start.16 = (f32[2,2,4,128]{3,2,1,0:T(4,128)S(1)}, f32[2,2,4,128]{3,2,1,0:T(4,128)S(1)}, u32[]{:S(2)}, u32[]{:S(2)}) collective-permute-start(f32[2,2,4,128]{3,2,1,0:T(4,128)S(1)} %maximum_add_fusion), channel_id=1, source_target_pairs={{0,32},{16,48},{32,0},{48,16},{1,33},{17,49},{33,1},{49,17},{2,34}... | collective-permute-start | bytes 24584 | tf_op jit(solution)/shard_map/totals/ppermute | solution.py:20
  67.3 3.8 %collective-permute-start.17 = (f32[2,2,4,128]{3,2,1,0:T(4,128)S(1)}, f32[2,2,4,128]{3,2,1,0:T(4,128)S(1)}, u32[]{:S(2)}, u32[]{:S(2)}) collective-permute-start(f32[2,2,4,128]{3,2,1,0:T(4,128)S(1)} %maximum_add_fusion), channel_id=1, source_target_pairs={{0,48},{16,0},{32,16},{48,32},{1,49},{17,1},{33,17},{49,33},{2,50}... | collective-permute-start | bytes 24584 | tf_op jit(solution)/shard_map/totals/ppermute | solution.py:20
  69.6 3.7 %collective-permute-start.15 = (f32[2,2,4,128]{3,2,1,0:T(4,128)S(1)}, f32[2,2,4,128]{3,2,1,0:T(4,128)S(1)}, u32[]{:S(2)}, u32[]{:S(2)}) collective-permute-start(f32[2,2,4,128]{3,2,1,0:T(4,128)S(1)} %maximum_add_fusion), channel_id=1, source_target_pairs={{0,16},{16,32},{32,48},{48,0},{1,17},{17,33},{33,49},{49,1},{2,18}... | collective-permute-start | bytes 24584 | tf_op jit(solution)/shard_map/totals/ppermute | solution.py:20
  76.9 26.7 %collective-permute-start.22 = (f32[4,128,512]{2,1,0:T(8,128)}, f32[4,128,512]{2,1,0:T(8,128)}, u32[]{:S(2)}, u32[]{:S(2)}) collective-permute-start(f32[4,128,512]{2,1,0:T(8,128)} %fusion.68), channel_id=1, source_target_pairs={{0,64},{64,0},{1,65},{65,1},{2,66},{66,2},{3,67},{67,3},{4,68},{68... | collective-permute-start | bytes 3145736 | tf_op jit(solution)/shard_map/pull/ppermute | solution.py:20
  94.1 2.0 %collective-permute-start.29 = (bf16[64,8,512]{2,1,0:T(8,128)(2,1)S(1)}, bf16[64,8,512]{2,1,0:T(8,128)(2,1)S(1)}, u32[]{:S(2)}, u32[]{:S(2)}) collective-permute-start(bf16[64,8,512]{2,1,0:T(8,128)(2,1)S(1)} %fusion.18), channel_id=1, source_target_pairs={{0,64},{64,0},{1,65},{65,1},{2,66},{66,2},{3,67},{67,3},{4,68},{68... | collective-permute-start | bytes 1572872 | tf_op jit(solution)/shard_map/head/ppermute | solution.py:20
  98.3 30.0 %all-to-all-start = ((bf16[64,8,512]{2,1,0:T(8,128)(2,1)}), bf16[64,8,512]{2,1,0:T(8,128)(2,1)S(1)}, u32[]{:S(2)}, u32[]{:S(2)}) async-start(bf16[64,8,512]{2,1,0:T(8,128)(2,1)} %fusion.14), calls=%async_computation | async-start | bytes 1048576 | tf_op jit(solution)/shard_map/head/all_to_all | solution.py:145
  105.2 7.5 %collective-permute-start.23 = (bf16[128,512]{1,0:T(8,128)(2,1)S(1)}, bf16[128,512]{1,0:T(8,128)(2,1)S(1)}, u32[]{:S(2)}, u32[]{:S(2)}) collective-permute-start(bf16[128,512]{1,0:T(8,128)(2,1)S(1)} %get-tuple-element.14), channel_id=1, source_target_pairs={{0,48},{16,0},{32,16},{48,32},{1,49},{17,1},{33,17},{49,33},{2,50}... | collective-permute-start | bytes 393224 | tf_op jit(solution)/shard_map/slopes/ppermute | solution.py:20
  107.7 8.4 %collective-permute-start.24 = (bf16[128,512]{1,0:T(8,128)(2,1)S(1)}, bf16[128,512]{1,0:T(8,128)(2,1)S(1)}, u32[]{:S(2)}, u32[]{:S(2)}) collective-permute-start(bf16[128,512]{1,0:T(8,128)(2,1)S(1)} %get-tuple-element.16), channel_id=1, source_target_pairs={{0,32},{16,48},{32,0},{48,16},{1,33},{17,49},{33,1},{49,17},{2,34}... | collective-permute-start | bytes 393224 | tf_op jit(solution)/shard_map/slopes/ppermute | solution.py:20
  108.1 13.6 %collective-permute-start.25 = (bf16[128,512]{1,0:T(8,128)(2,1)S(1)}, bf16[128,512]{1,0:T(8,128)(2,1)S(1)}, u32[]{:S(2)}, u32[]{:S(2)}) collective-permute-start(bf16[128,512]{1,0:T(8,128)(2,1)S(1)} %get-tuple-element.15), channel_id=1, source_target_pairs={{0,16},{16,32},{32,48},{48,0},{1,17},{17,33},{33,49},{49,1},{2,18}... | collective-permute-start | bytes 393224 | tf_op jit(solution)/shard_map/slopes/ppermute | solution.py:20
  122.0 7.2 %collective-permute-start.26 = (bf16[32,512]{1,0:T(8,128)(2,1)S(1)}, bf16[32,512]{1,0:T(8,128)(2,1)S(1)}, u32[]{:S(2)}, u32[]{:S(2)}) collective-permute-start(bf16[32,512]{1,0:T(8,128)(2,1)S(1)} %get-tuple-element.26), channel_id=1, source_target_pairs={{0,12},{4,0},{8,4},{12,8},{1,13},{5,1},{9,5},{13,9},{2,14},{6,2},{... | collective-permute-start | bytes 98312 | tf_op jit(solution)/shard_map/route_back/ppermute | solution.py:20
  124.9 6.8 %collective-permute-start.27 = (bf16[32,512]{1,0:T(8,128)(2,1)S(1)}, bf16[32,512]{1,0:T(8,128)(2,1)S(1)}, u32[]{:S(2)}, u32[]{:S(2)}) collective-permute-start(bf16[32,512]{1,0:T(8,128)(2,1)S(1)} %get-tuple-element.25), channel_id=1, source_target_pairs={{0,8},{4,12},{8,0},{12,4},{1,9},{5,13},{9,1},{13,5},{2,10},{6,14},... | collective-permute-start | bytes 98312 | tf_op jit(solution)/shard_map/route_back/ppermute | solution.py:20
  126.4 5.3 %collective-permute-start.28 = (bf16[32,512]{1,0:T(8,128)(2,1)S(1)}, bf16[32,512]{1,0:T(8,128)(2,1)S(1)}, u32[]{:S(2)}, u32[]{:S(2)}) collective-permute-start(bf16[32,512]{1,0:T(8,128)(2,1)S(1)} %get-tuple-element.24), channel_id=1, source_target_pairs={{0,4},{4,8},{8,12},{12,0},{1,5},{5,9},{9,13},{13,1},{2,6},{6,10},{... | collective-permute-start | bytes 98312 | tf_op jit(solution)/shard_map/route_back/ppermute | solution.py:20
  128.4 4.6 %collective-permute-start.30 = (f32[8,512]{1,0:T(8,128)S(1)}, f32[8,512]{1,0:T(8,128)S(1)}, u32[]{:S(2)}, u32[]{:S(2)}) collective-permute-start(f32[8,512]{1,0:T(8,128)S(1)} %convert_reduce_fusion), channel_id=1, source_target_pairs={{0,128},{128,0},{1,129},{129,1},{2,130},{130,2},{3,131},{131,3},{4... | collective-permute-start | bytes 49160 | tf_op jit(solution)/shard_map/head/ppermute | solution.py:20
  (8 other events, 56.2 us)
